TPU v7x, 32 devices: a whole 2x2x4 slice. The times are simulated.
32 devices in a mesh: dp: 8 (over y, x, core), own: 4 (over z).
Axes of the slice: x: 2, y: 2, z: 4, core: 2. Of those that a mesh axis runs over, the one named last changes fastest.
Arguments:
- grads: bfloat16 [8, 6, 8192, 128], P('dp', None, 'own'), may hold values from -6 to 6
- proj: bfloat16 [4, 3, 8192, 1024], P('own', None, 'dp'), may hold values from -0.0625 to 0.0625
- moment1: float32 [4, 3, 1024, 128], P('own', None, 'dp'), may hold values from -24 to 24
- moment2: float32 [4, 3, 1024, 128], P('own', None, 'dp'), may hold values from 0.05 to 5
- plan: int32 [6], replicated, may hold values from 0 to 3, as said below
Outputs:
- update: bfloat16 [6, 8192, 128], P(None, 'own')
- new_moment1: float32 [4, 3, 1024, 128], P('own', None, 'dp')
- new_moment2: float32 [4, 3, 1024, 128], P('own', None, 'dp')
Inputs may be any that keep to these rules, and one draw needn't show every extreme that they name: `plan`: no owner is named more than 3 times, and some owner is named exactly 3 times.
All inputs are finite; a program needn't handle non-finite values.
Results may differ from a plain program's by a relative error of at most 0.015.
Values may be sent and summed in bfloat16 or wider, within the bound.
A program may use at most 64 MiB of HBM per device.

v0:
```python
import jax
import jax.numpy as jnp
from jax import lax
from jax.sharding import PartitionSpec as P

beta_one = 0.9
beta_two = 0.999
adam_eps = 1e-08
norm_eps = 1e-06
correct_one = 1.0 - 0.9**10
correct_two = 1.0 - 0.999**10


def slot_selector(plan, owner_count, capacity):
    matrices = plan.shape[0]
    places = jnp.arange(owner_count * capacity, dtype=jnp.int32)
    owners = places // capacity
    within = places % capacity
    index = jnp.arange(matrices, dtype=jnp.int32)
    before = jnp.sum(
        ((plan[None, :] == plan[:, None]) & (index[None, :] < index[:, None])).astype(jnp.int32),
        axis=1,
    )
    chosen = (plan[None, :] == owners[:, None]) & (before[None, :] == within[:, None])
    return chosen.astype(jnp.bfloat16)


def adam_moments(rank_share, first_old, second_old):
    first_new = beta_one * first_old + (1.0 - beta_one) * rank_share
    second_new = beta_two * second_old + (1.0 - beta_two) * rank_share * rank_share
    adam_step = first_new / correct_one / (jnp.sqrt(second_new / correct_two) + adam_eps)
    return (first_new, second_new, adam_step.astype(jnp.bfloat16))


def local(grads, proj, moment1, moment2, plan):
    owner_count = lax.axis_size("own")
    replica_count = lax.axis_size("dp")
    capacity = proj.shape[1]
    own_rows = grads.shape[2]
    columns = grads.shape[3]
    rank_rows = moment1.shape[2]
    selector = slot_selector(plan, owner_count, capacity)
    outgoing = jnp.einsum(
        "sj,jdc->sdc", selector, grads[0], preferred_element_type=jnp.float32
    ).astype(jnp.bfloat16)
    group_ratio = replica_count // owner_count
    piece_rows = own_rows // replica_count
    blocked = outgoing.reshape(owner_count * capacity, replica_count, piece_rows, columns)
    pieces = lax.psum_scatter(blocked, "dp", scatter_dimension=1, tiled=True).astype(jnp.float32)
    pieces = pieces.reshape(owner_count, capacity, piece_rows, columns)
    routed = lax.all_to_all(
        pieces.astype(jnp.bfloat16), "own", split_axis=0, concat_axis=0, tiled=True
    ).astype(pieces.dtype)
    span_pos = lax.axis_index("dp") // owner_count
    marker = (jnp.arange(group_ratio, dtype=jnp.int32) == span_pos).astype(jnp.float32)
    placed = routed[:, None] * marker[None, :, None, None, None]
    placed = placed.reshape(replica_count, capacity, piece_rows, columns)
    received = lax.all_to_all(
        placed.astype(jnp.bfloat16), "dp", split_axis=0, concat_axis=0, tiled=True
    ).astype(placed.dtype)
    received = received.reshape(group_ratio, owner_count, capacity, piece_rows, columns)
    mine = lax.axis_index("dp") % group_ratio
    kept = lax.dynamic_index_in_dim(received, mine, 0, keepdims=False)
    summed = jnp.transpose(kept, (1, 0, 2, 3)).reshape(capacity, owner_count * piece_rows, columns)
    grad_half = summed.astype(jnp.bfloat16)
    projection = proj[0]
    partial_value = jnp.einsum(
        "kdr,kdc->krc", projection, grad_half, preferred_element_type=jnp.float32
    )
    first_old = moment1[0]
    second_old = moment2[0]
    rank_full = lax.psum(partial_value.astype(jnp.bfloat16), "dp").astype(jnp.float32)
    rank_start = lax.axis_index("dp") * rank_rows
    rank_share = lax.dynamic_slice_in_dim(rank_full, rank_start, rank_rows, 1)
    first_new, second_new, adam_half = adam_moments(rank_share, first_old, second_old)
    adam_full = lax.all_gather(adam_half, "dp", axis=1, tiled=True)
    rank_half = rank_full.astype(jnp.bfloat16)
    grad_norms = jnp.sum(rank_full * rank_full, axis=1)
    adam_wide = adam_full.astype(jnp.float32)
    step_norms = jnp.sum(adam_wide * adam_wide, axis=1)
    column_scale = jnp.sqrt(step_norms) / (jnp.sqrt(grad_norms) + norm_eps)
    combined = (adam_wide - column_scale[:, None, :] * rank_half.astype(jnp.float32)).astype(
        jnp.bfloat16
    )
    update_full = (
        jnp.einsum("kdr,krc->kdc", projection, combined, preferred_element_type=jnp.float32)
        + column_scale[:, None, :] * summed
    )
    update_half = update_full.astype(jnp.bfloat16)
    gathered = lax.all_gather(update_half, "dp", axis=1, tiled=True)
    gathered = gathered.reshape(capacity, owner_count, own_rows, columns)
    returned = lax.all_to_all(gathered, "own", split_axis=1, concat_axis=0, tiled=True)
    slot_rows = returned.reshape(owner_count * capacity, own_rows, columns)
    update = jnp.einsum(
        "sj,sdc->jdc", selector, slot_rows, preferred_element_type=jnp.float32
    ).astype(jnp.bfloat16)
    return (update, first_new[None], second_new[None])


def solution(mesh):
    return jax.shard_map(
        local,
        mesh=mesh,
        in_specs=(
            P("dp", None, "own", None),
            P("own", None, "dp", None),
            P("own", None, "dp", None),
            P("own", None, "dp", None),
            P(),
        ),
        out_specs=(P(None, "own", None), P("own", None, "dp", None), P("own", None, "dp", None)),
        check_vma=False,
    )
```

profile of v0, /device:TPU:0, one launch (start us, length us, event | category | flops | bytes accessed | tf_op | source)
XLA Modules:
  0.0 447.2 jit_solution(17571062850924733432)
XLA Ops:
  7.2 0.0 copy-start
  7.2 0.0 reduce-scatter.2.cloned.1.call-start
  7.2 1.0 convert_reduce_fusion
  8.2 0.8 copy-done
  9.1 13.2 %convolution_convert_fusion = bf16[12,2048,128]{2,0,1:T(8,128)(2,1)S(1)} fusion(bf16[6,2048,128]{2,1,0:T(8,128)(2,1)S(1)} %bitcast.60, s32[12]{0:T(128)S(1)} %get-tuple-element.18, s32[12]{0:T(128)S(1)} %get-tuple-element.19, s32[6]{0:T(128)S(1)} %convert_reduce_fusion, s32[6]{0:T(128)} %param.9), kind=kOutput, calls=%fused_computation.2 | convolution fusion | flops 40894680 | bytes 9437328 | tf_op jit(solution)/shard_map/sj,jdc->sdc/dot_general | solution.py:43
  22.3 4.4 copy.37
  26.8 0.0 reduce-scatter.2.cloned.1.call-update
  26.8 64.6 %reduce-scatter.2.cloned.1.call-done = bf16[12,1,256,128]{3,2,0,1:T(8,128)(2,1)} async-done(((bf16[12,8,256,128]{3,2,0,1:T(8,128)(2,1)}), bf16[12,1,256,128]{3,2,0,1:T(8,128)(2,1)}) %reduce-scatter.2.cloned.1.call-update) | async-done | bytes 786448 | tf_op jit(solution)/shard_map/reduce_scatter | solution.py:49
  91.4 4.6 %all-to-all-start = ((bf16[4,3,256,128]{3,2,1,0:T(8,128)(2,1)}), bf16[4,3,256,128]{3,2,1,0:T(8,128)(2,1)S(1)}, u32[]{:S(2)}, u32[]{:S(2)}) async-start(bf16[4,3,256,128]{3,2,1,0:T(8,128)(2,1)} %bitcast.63), calls=%async_computation.1 | async-start | bytes 1572864 | tf_op jit(solution)/shard_map/all_to_all | solution.py:51
  96.0 0.1 mul.82
  96.1 19.8 %all-to-all-done = bf16[4,3,256,128]{3,2,1,0:T(8,128)(2,1)S(1)} async-done(((bf16[4,3,256,128]{3,2,1,0:T(8,128)(2,1)}), bf16[4,3,256,128]{3,2,1,0:T(8,128)(2,1)S(1)}, u32[]{:S(2)}, u32[]{:S(2)}) %all-to-all-start) | async-done | bytes 786464 | tf_op jit(solution)/shard_map/all_to_all | solution.py:51
  116.0 0.1 convert_element_type.58
  116.1 1.6 fusion.7
  117.7 3.6 all-to-all-start.1
  121.3 0.0 all-reduce.2.cloned.1.call-start
  121.3 20.9 %all-to-all-done.1 = bf16[8,3,256,128]{3,2,1,0:T(8,128)(2,1)S(1)} async-done(((bf16[8,3,256,128]{3,2,1,0:T(8,128)(2,1)}), bf16[8,3,256,128]{3,2,1,0:T(8,128)(2,1)S(1)}, u32[]{:S(2)}, u32[]{:S(2)}) %all-to-all-start.1) | async-done | bytes 1572896 | tf_op jit(solution)/shard_map/all_to_all | solution.py:58
  142.2 0.1 convert_bitcast_fusion
  142.4 0.8 copy.38
  143.2 0.8 reshape.73
  144.0 0.0 copy-start.3
  144.0 0.0 copy-start.4
  144.0 4.7 %fusion.19 = bf16[3,1024,128]{1,2,0:T(8,128)(2,1)} fusion(bf16[1,3,1024,1024]{3,2,1,0:T(8,128)(2,1)} %param.6, f32[3,1024,128]{1,2,0:T(8,128)S(1)} %reshape.73), kind=kOutput, calls=%fused_computation.20 | convolution fusion | flops 806092800 | bytes 8650752 | tf_op jit(solution)/shard_map/kdr,kdc->krc/dot_general | solution.py:67
  148.8 0.0 all-reduce.2.cloned.1.call-update
  148.8 0.0 all-gather.2.cloned.1.call-start
  148.8 0.0 copy-done.3
  148.8 0.1 copy.35
  149.0 0.0 copy-done.4
  149.0 0.1 copy.39
  149.1 52.7 %all-reduce.2.cloned.1.call-done = bf16[3,1024,128]{1,2,0:T(8,128)(2,1)} async-done(((bf16[3,1024,128]{1,2,0:T(8,128)(2,1)}), bf16[3,1024,128]{1,2,0:T(8,128)(2,1)}) %all-reduce.2.cloned.1.call-update) | async-done | bytes 786448 | tf_op jit(solution)/shard_map/psum | solution.py:72
  201.8 0.0 copy-start.2
  201.8 1.4 convert_element_type.64
  203.2 0.2 fusion.28
  203.4 10.0 %all_gather.6 = bf16[3,1024,128]{1,2,0:T(8,128)(2,1)S(1)} all-gather(bf16[3,128,128]{1,2,0:T(8,128)(2,1)S(1)} %get-tuple-element.16), channel_id=1, replica_groups=mesh['dp'=8,'own'=4] {'dp'}, dimensions={1}, use_global_device_ids=true | all-gather | bytes 884736 | tf_op jit(solution)/shard_map/all_gather | solution.py:76
  213.4 0.2 fusion.11
  213.6 0.0 copy-done.2
  213.6 0.2 multiply_reduce_fusion
  213.9 5.9 %fusion.13 = bf16[3,1024,128]{1,2,0:T(8,128)(2,1)} fusion(f32[3,1024,128]{1,2,0:T(8,128)S(1)} %reshape.73, bf16[1,3,1024,1024]{3,2,1,0:T(8,128)(2,1)} %param.6, bf16[3,1024,128]{1,2,0:T(8,128)(2,1)S(1)} %all_gather.6, f32[3,128]{1,0:T(4,128)S(1)} %add_divide_fusion, bf16[3,1024,128]{1,2,0:T(8,128)(2,1)S(1)} %copy-done.2), kind=kOutput, calls=%fused_computation.17 | convolution fusion | flops 808452096 | bytes 10225152 | tf_op jit(solution)/shard_map/kdr,krc->kdc/dot_general | solution.py:86
  219.8 0.0 all-gather.2.cloned.1.call-update
  219.8 45.6 %all-gather.2.cloned.1.call-done = bf16[3,8192,128]{1,2,0:T(8,128)(2,1)} async-done(((bf16[3,1024,128]{1,2,0:T(8,128)(2,1)}), bf16[3,8192,128]{1,2,0:T(8,128)(2,1)}) %all-gather.2.cloned.1.call-update) | async-done | bytes 6291472 | tf_op jit(solution)/shard_map/all_gather | solution.py:90
  265.4 11.1 %reshape.74 = bf16[3,4,2048,128]{2,1,3,0:T(4,128)(2,1)} reshape(bf16[3,8192,128]{1,2,0:T(8,128)(2,1)} %all-gather.2.cloned.1.call-done) | data formatting | bytes 12582912 | tf_op jit(solution)/shard_map/reshape | solution.py:91
  276.5 11.2 %copy.40 = bf16[3,4,2048,128]{3,2,0,1:T(8,128)(2,1)} copy(bf16[3,4,2048,128]{2,1,3,0:T(4,128)(2,1)} %reshape.74) | data formatting | bytes 12582912 | tf_op jit(solution)/shard_map/reshape | solution.py:91
  287.7 0.0 copy-start.5
  287.7 5.4 %all-to-all-start.2 = ((bf16[3,4,2048,128]{3,2,0,1:T(8,128)(2,1)}), bf16[3,4,2048,128]{3,2,0,1:T(8,128)(2,1)}, u32[]{:S(2)}, u32[]{:S(2)}) async-start(bf16[3,4,2048,128]{3,2,0,1:T(8,128)(2,1)} %copy.40), calls=%async_computation.3 | async-start | bytes 12582912 | tf_op jit(solution)/shard_map/all_to_all | solution.py:92
  293.1 0.8 copy.43
  293.9 0.8 copy.44
  294.7 137.2 %all-to-all-done.2 = bf16[3,4,2048,128]{3,2,0,1:T(8,128)(2,1)} async-done(((bf16[3,4,2048,128]{3,2,0,1:T(8,128)(2,1)}), bf16[3,4,2048,128]{3,2,0,1:T(8,128)(2,1)}, u32[]{:S(2)}, u32[]{:S(2)}) %all-to-all-start.2) | async-done | bytes 6291488 | tf_op jit(solution)/shard_map/all_to_all | solution.py:92
  431.9 0.0 copy-done.5
  431.9 0.0 copy-start.1
  431.9 6.7 %fusion.8 = bf16[6,2048,128]{2,0,1:T(8,128)(2,1)S(1)} fusion(bf16[12,2048,128]{2,1,0:T(8,128)(2,1)} %bitcast.15, s32[12]{0:T(128)S(1)} %get-tuple-element.18, s32[12]{0:T(128)S(1)} %get-tuple-element.19, s32[6]{0:T(128)S(1)} %convert_reduce_fusion, s32[6]{0:T(128)S(1)} %copy-done.5), kind=kOutput, calls=%fused_computation.10 | convolution fusion | flops 39321816 | bytes 9437328 | tf_op jit(solution)/shard_map/sj,sdc->jdc/dot_general | solution.py:94
  438.6 2.1 copy.42
  440.7 0.0 copy-done.1
  (4 shorter events, 0.0 us)
Async XLA Ops:
  7.2 1.9 copy-start
  7.2 84.2 %reduce-scatter.2.cloned.1.call-start = ((), (), s32[]{:S(2)}) async-start(), calls=%async_computation.4 | async-start | bytes 7077888 | tf_op jit(solution)/shard_map/reduce_scatter | solution.py:49
  91.4 24.6 %all-to-all-start = ((bf16[4,3,256,128]{3,2,1,0:T(8,128)(2,1)}), bf16[4,3,256,128]{3,2,1,0:T(8,128)(2,1)S(1)}, u32[]{:S(2)}, u32[]{:S(2)}) async-start(bf16[4,3,256,128]{3,2,1,0:T(8,128)(2,1)} %bitcast.63), calls=%async_computation.1 | async-start | bytes 1572864 | tf_op jit(solution)/shard_map/all_to_all | solution.py:51
  117.7 24.5 %all-to-all-start.1 = ((bf16[8,3,256,128]{3,2,1,0:T(8,128)(2,1)}), bf16[8,3,256,128]{3,2,1,0:T(8,128)(2,1)S(1)}, u32[]{:S(2)}, u32[]{:S(2)}) async-start(bf16[8,3,256,128]{3,2,1,0:T(8,128)(2,1)} %fusion.7), calls=%async_computation.2 | async-start | bytes 3145728 | tf_op jit(solution)/shard_map/all_to_all | solution.py:58
  121.3 80.5 %all-reduce.2.cloned.1.call-start = ((), (), s32[]{:S(2)}) async-start(), calls=%async_computation.5 | async-start | bytes 1572864 | tf_op jit(solution)/shard_map/psum | solution.py:72
  144.0 4.8 %copy-start.3 = (f32[1,3,128,128]{3,2,1,0:T(8,128)S(1)}, f32[1,3,128,128]{3,2,1,0:T(8,128)}, u32[]{:S(2)}) copy-start(f32[1,3,128,128]{3,2,1,0:T(8,128)} %param.7) | copy-start | bytes 589828
  144.0 4.9 %copy-start.4 = (f32[1,3,128,128]{3,2,1,0:T(8,128)S(1)}, f32[1,3,128,128]{3,2,1,0:T(8,128)}, u32[]{:S(2)}) copy-start(f32[1,3,128,128]{3,2,1,0:T(8,128)} %param.8) | copy-start | bytes 589828
  148.8 116.6 %all-gather.2.cloned.1.call-start = ((), (), s32[]{:S(2)}) async-start(), calls=%async_computation.6 | async-start | bytes 7077888 | tf_op jit(solution)/shard_map/all_gather | solution.py:90
  201.8 11.8 %copy-start.2 = (bf16[3,1024,128]{1,2,0:T(8,128)(2,1)S(1)}, bf16[3,1024,128]{1,2,0:T(8,128)(2,1)}, u32[]{:S(2)}) copy-start(bf16[3,1024,128]{1,2,0:T(8,128)(2,1)} %all-reduce.2.cloned.1.call-done) | copy-start | bytes 2359300
  287.7 144.2 %copy-start.5 = (s32[6]{0:T(128)S(1)}, s32[6]{0:T(128)}, u32[]{:S(2)}) copy-start(s32[6]{0:T(128)} %param.9) | copy-start | bytes 76
  287.7 144.2 %all-to-all-start.2 = ((bf16[3,4,2048,128]{3,2,0,1:T(8,128)(2,1)}), bf16[3,4,2048,128]{3,2,0,1:T(8,128)(2,1)}, u32[]{:S(2)}, u32[]{:S(2)}) async-start(bf16[3,4,2048,128]{3,2,0,1:T(8,128)(2,1)} %copy.40), calls=%async_computation.3 | async-start | bytes 12582912 | tf_op jit(solution)/shard_map/all_to_all | solution.py:92
  431.9 8.7 %copy-start.1 = (bf16[1,6,2048,128]{3,2,1,0:T(8,128)(2,1)S(1)}, bf16[1,6,2048,128]{3,2,1,0:T(8,128)(2,1)}, u32[]{:S(2)}) copy-start(bf16[1,6,2048,128]{3,2,1,0:T(8,128)(2,1)} %param.5) | copy-start | bytes 9437188
Sparse Core Ops, SparseCore 0:
  26.9 64.4 reduce-scatter.1
  148.9 52.8 all-reduce.1
  219.9 45.3 all-gather.1
where the time goes:
time: 448 us; the launch traced here: 447 us
  waiting for transfers between devices  341 us (76%)
  local copies, waits for them, and re-layouts  33.4 us (7%)
  matrix products  30.5 us (7%)
  between operations  13.9 us (3%)
  starting transfers between devices  13.7 us (3%)
  blocking collectives  10 us (2%)
  other arithmetic  4.87 us (1%)
    all_to_all x1, waiting for transfers between devices, local(): lax.all_to_all(gathered, 'own', split_axis=1, concat_axis=0, tiled=True)  137 us
    reduce_scatter x1, waiting for transfers between devices, local(): lax.psum_scatter(blocked, 'dp', scatter_dimension=1, tiled=True)  64.6 us
    psum x1, waiting for transfers between devices, local(): lax.psum(partial_value.astype(jnp.bfloat16), 'dp').astype(jnp.float32)  52.7 us
    all_gather x1, waiting for transfers between devices, local(): gathered = lax.all_gather(update_half, 'dp', axis=1, tiled=True)  45.6 us
    reshape x2, local copies, waits for them, and re-layouts, local(): gathered = gathered.reshape(capacity, owner_count, own_rows, columns)  22.4 us
    all_to_all x1, waiting for transfers between devices, local(): lax.all_to_all(placed.astype(jnp.bfloat16), 'dp', split_axis=0, concat_ax...  20.9 us
    all_to_all x1, waiting for transfers between devices, local(): lax.all_to_all(pieces.astype(jnp.bfloat16), 'own', split_axis=0, concat_a...  19.8 us
    dot_general x1, matrix products, local(): jnp.einsum('sj,jdc->sdc', selector, grads[0], preferred_element_type=jnp....  13.2 us
  transfers between devices with their start and end apart: 6, of which 6 were waited for; matrix products, arithmetic and copies ran while one was open for 0% of the time, Pallas kernels for 0%

commit v1 on v0

--- a/solution.py
+++ b/solution.py
@@ -89,7 +89,9 @@
     update_half = update_full.astype(jnp.bfloat16)
     gathered = lax.all_gather(update_half, "dp", axis=1, tiled=True)
     gathered = gathered.reshape(capacity, owner_count, own_rows, columns)
-    returned = lax.all_to_all(gathered, "own", split_axis=1, concat_axis=0, tiled=True)
+    parts = jnp.split(gathered, lax.axis_size("own"), axis=1)
+    got = lax.all_to_all(jnp.stack(parts), "own", 0, 0)
+    returned = jnp.concatenate(got, axis=0)
     slot_rows = returned.reshape(owner_count * capacity, own_rows, columns)
     update = jnp.einsum(
         "sj,sdc->jdc", selector, slot_rows, preferred_element_type=jnp.float32

time: 448 us -> 494 us (1.10)
  local copies, waits for them, and re-layouts: 33.4 us -> 72.7 us
  other arithmetic: 4.87 us -> 11.4 us
    unnamed x17 -> x21, local copies, waits for them, and re-layouts: 4.83 us -> 34.6 us
    split x0 -> x1, local copies, waits for them, and re-layouts: none -> 20.8 us  [local(): parts = jnp.split(gathered, lax.axis_size('own'), axis=1)]
    reshape x2 -> x1, local copies, waits for them, and re-layouts: 22.4 us -> 11.1 us  [local(): gathered = gathered.reshape(capacity, owner_count, own_rows, columns)]
    another operation x0 -> x1, other arithmetic: none -> 6.49 us  [local(): got = lax.all_to_all(jnp.stack(parts), 'own', 0, 0)]
where the time goes in v1:
time: 494 us; the launch traced here: 493 us
  waiting for transfers between devices  341 us (69%)
  local copies, waits for them, and re-layouts  72.7 us (15%)
  matrix products  30.5 us (6%)
  between operations  13.9 us (3%)
  starting transfers between devices  13.7 us (3%)
  other arithmetic  11.4 us (2%)
  blocking collectives  10 us (2%)
    all_to_all x1, waiting for transfers between devices, local(): got = lax.all_to_all(jnp.stack(parts), 'own', 0, 0)  137 us
    reduce_scatter x1, waiting for transfers between devices, local(): lax.psum_scatter(blocked, 'dp', scatter_dimension=1, tiled=True)  64.6 us
    psum x1, waiting for transfers between devices, local(): lax.psum(partial_value.astype(jnp.bfloat16), 'dp').astype(jnp.float32)  52.8 us
    all_gather x1, waiting for transfers between devices, local(): gathered = lax.all_gather(update_half, 'dp', axis=1, tiled=True)  45.6 us
    unnamed x21, local copies, waits for them, and re-layouts  34.6 us
    all_to_all x1, waiting for transfers between devices, local(): lax.all_to_all(placed.astype(jnp.bfloat16), 'dp', split_axis=0, concat_ax...  20.9 us
    split x1, local copies, waits for them, and re-layouts, local(): parts = jnp.split(gathered, lax.axis_size('own'), axis=1)  20.8 us
    all_to_all x1, waiting for transfers between devices, local(): lax.all_to_all(pieces.astype(jnp.bfloat16), 'own', split_axis=0, concat_a...  19.8 us
  transfers between devices with their start and end apart: 6, of which 6 were waited for; matrix products, arithmetic and copies ran while one was open for 0% of the time, Pallas kernels for 0%

profile of v1, /device:TPU:0, one launch (start us, length us, event | category | flops | bytes accessed | tf_op | source)
XLA Modules:
  0.0 493.1 jit_solution(3795367024000019803)
XLA Ops:
  7.2 0.0 copy-start
  7.2 0.0 reduce-scatter.2.cloned.1.call-start
  7.2 1.0 convert_reduce_fusion
  8.2 0.8 copy-done
  9.1 13.2 %convolution_convert_fusion = bf16[12,2048,128]{2,0,1:T(8,128)(2,1)S(1)} fusion(bf16[6,2048,128]{2,1,0:T(8,128)(2,1)S(1)} %bitcast.60, s32[12]{0:T(128)S(1)} %get-tuple-element.22, s32[12]{0:T(128)S(1)} %get-tuple-element.23, s32[6]{0:T(128)S(1)} %convert_reduce_fusion, s32[6]{0:T(128)} %param.9), kind=kOutput, calls=%fused_computation.2 | convolution fusion | flops 40894680 | bytes 9437328 | tf_op jit(solution)/shard_map/sj,jdc->sdc/dot_general | solution.py:43
  22.3 4.4 copy.46
  26.8 0.0 reduce-scatter.2.cloned.1.call-update
  26.8 64.6 %reduce-scatter.2.cloned.1.call-done = bf16[12,1,256,128]{3,2,0,1:T(8,128)(2,1)} async-done(((bf16[12,8,256,128]{3,2,0,1:T(8,128)(2,1)}), bf16[12,1,256,128]{3,2,0,1:T(8,128)(2,1)}) %reduce-scatter.2.cloned.1.call-update) | async-done | bytes 786448 | tf_op jit(solution)/shard_map/reduce_scatter | solution.py:49
  91.4 4.6 all-to-all-start
  96.0 0.1 mul.82
  96.1 19.8 %all-to-all-done = bf16[4,3,256,128]{3,2,1,0:T(8,128)(2,1)S(1)} async-done(((bf16[4,3,256,128]{3,2,1,0:T(8,128)(2,1)}), bf16[4,3,256,128]{3,2,1,0:T(8,128)(2,1)S(1)}, u32[]{:S(2)}, u32[]{:S(2)}) %all-to-all-start) | async-done | bytes 786464 | tf_op jit(solution)/shard_map/all_to_all | solution.py:51
  116.0 0.1 convert_element_type.58
  116.1 1.6 fusion.7
  117.7 3.6 all-to-all-start.1
  121.3 0.0 all-reduce.2.cloned.1.call-start
  121.3 20.9 %all-to-all-done.1 = bf16[8,3,256,128]{3,2,1,0:T(8,128)(2,1)S(1)} async-done(((bf16[8,3,256,128]{3,2,1,0:T(8,128)(2,1)}), bf16[8,3,256,128]{3,2,1,0:T(8,128)(2,1)S(1)}, u32[]{:S(2)}, u32[]{:S(2)}) %all-to-all-start.1) | async-done | bytes 1572896 | tf_op jit(solution)/shard_map/all_to_all | solution.py:58
  142.2 0.1 convert_bitcast_fusion
  142.4 0.8 copy.47
  143.2 0.8 reshape.69
  144.0 0.0 copy-start.3
  144.0 0.0 copy-start.4
  144.0 4.7 fusion.19
  148.7 0.0 all-reduce.2.cloned.1.call-update
  148.8 0.0 all-gather.2.cloned.1.call-start
  148.8 0.0 copy-done.3
  148.8 0.1 copy.44
  149.0 0.0 copy-done.4
  149.0 0.1 copy.48
  149.1 52.8 %all-reduce.2.cloned.1.call-done = bf16[3,1024,128]{1,2,0:T(8,128)(2,1)} async-done(((bf16[3,1024,128]{1,2,0:T(8,128)(2,1)}), bf16[3,1024,128]{1,2,0:T(8,128)(2,1)}) %all-reduce.2.cloned.1.call-update) | async-done | bytes 786448 | tf_op jit(solution)/shard_map/psum | solution.py:72
  201.9 0.0 copy-start.2
  201.9 1.4 convert_element_type.64
  203.2 0.2 fusion.28
  203.4 10.0 %all_gather.6 = bf16[3,1024,128]{1,2,0:T(8,128)(2,1)S(1)} all-gather(bf16[3,128,128]{1,2,0:T(8,128)(2,1)S(1)} %get-tuple-element.20), channel_id=1, replica_groups=mesh['dp'=8,'own'=4] {'dp'}, dimensions={1}, use_global_device_ids=true | all-gather | bytes 884736 | tf_op jit(solution)/shard_map/all_gather | solution.py:76
  213.4 0.2 fusion.11
  213.7 0.0 copy-done.2
  213.7 0.2 multiply_reduce_fusion
  213.9 5.9 %fusion.13 = bf16[3,1024,128]{1,2,0:T(8,128)(2,1)} fusion(f32[3,1024,128]{1,2,0:T(8,128)S(1)} %reshape.69, bf16[1,3,1024,1024]{3,2,1,0:T(8,128)(2,1)} %param.6, bf16[3,1024,128]{1,2,0:T(8,128)(2,1)S(1)} %all_gather.6, f32[3,128]{1,0:T(4,128)S(1)} %add_divide_fusion, bf16[3,1024,128]{1,2,0:T(8,128)(2,1)S(1)} %copy-done.2), kind=kOutput, calls=%fused_computation.18 | convolution fusion | flops 808452096 | bytes 10225152 | tf_op jit(solution)/shard_map/kdr,krc->kdc/dot_general | solution.py:86
  219.8 0.0 all-gather.2.cloned.1.call-update
  219.8 45.6 %all-gather.2.cloned.1.call-done = bf16[3,8192,128]{1,2,0:T(8,128)(2,1)} async-done(((bf16[3,1024,128]{1,2,0:T(8,128)(2,1)}), bf16[3,8192,128]{1,2,0:T(8,128)(2,1)}) %all-gather.2.cloned.1.call-update) | async-done | bytes 6291472 | tf_op jit(solution)/shard_map/all_gather | solution.py:90
  265.4 11.1 %reshape.70 = bf16[3,4,2048,128]{2,1,3,0:T(4,128)(2,1)} reshape(bf16[3,8192,128]{1,2,0:T(8,128)(2,1)} %all-gather.2.cloned.1.call-done) | data formatting | bytes 12582912 | tf_op jit(solution)/shard_map/reshape | solution.py:91
  276.5 20.8 %fusion.40 = (bf16[3,1,2048,128]{2,1,3,0:T(2,128)(2,1)}, bf16[3,1,2048,128]{2,1,3,0:T(2,128)(2,1)}, bf16[3,1,2048,128]{2,1,3,0:T(2,128)(2,1)}, bf16[3,1,2048,128]{2,1,3,0:T(2,128)(2,1)S(1)}) fusion(bf16[3,4,2048,128]{2,1,3,0:T(4,128)(2,1)} %reshape.70), kind=kLoop, calls=%fused_computation.52 | loop fusion | bytes 12582912 | tf_op jit(solution)/shard_map/split | solution.py:92
  297.3 8.2 %copy.57 = bf16[3,1,2048,128]{3,2,0,1:T(8,128)(2,1)} copy(bf16[3,1,2048,128]{2,1,3,0:T(2,128)(2,1)} %get-tuple-element.15) | data formatting | bytes 3145728
  305.5 8.2 %copy.59 = bf16[3,1,2048,128]{3,2,0,1:T(8,128)(2,1)} copy(bf16[3,1,2048,128]{2,1,3,0:T(2,128)(2,1)} %get-tuple-element.16) | data formatting | bytes 3145728
  313.7 8.2 %copy.58 = bf16[3,1,2048,128]{3,2,0,1:T(8,128)(2,1)} copy(bf16[3,1,2048,128]{2,1,3,0:T(2,128)(2,1)} %get-tuple-element.17) | data formatting | bytes 3145728
  321.9 5.2 %copy.60 = bf16[3,1,2048,128]{3,2,0,1:T(8,128)(2,1)} copy(bf16[3,1,2048,128]{2,1,3,0:T(2,128)(2,1)S(1)} %get-tuple-element.18) | data formatting | bytes 3145728
  327.1 6.5 %pad_maximum_fusion = bf16[4,3,1,2048,128]{4,3,1,2,0:T(8,128)(2,1)} fusion(bf16[1,3,1,2048,128]{4,3,1,2,0:T(8,128)(2,1)} %bitcast.65, bf16[1,3,1,2048,128]{4,3,1,2,0:T(8,128)(2,1)} %bitcast.63, bf16[1,3,1,2048,128]{4,3,1,2,0:T(8,128)(2,1)} %bitcast.64, bf16[1,3,1,2048,128]{4,3,1,2,0:T(8,128)(2,1)} %bitcast.62), kind=kLoop, calls=%fused_computation.3 | loop fusion | flops 9437184 | bytes 12582912 | tf_op jit(solution)/shard_map/stack | solution.py:93
  333.6 0.0 copy-start.5
  333.6 5.4 %all-to-all-start.2 = ((bf16[4,3,1,2048,128]{4,3,1,2,0:T(8,128)(2,1)}), bf16[4,3,1,2048,128]{4,3,1,2,0:T(8,128)(2,1)}, u32[]{:S(2)}, u32[]{:S(2)}) async-start(bf16[4,3,1,2048,128]{4,3,1,2,0:T(8,128)(2,1)} %pad_maximum_fusion), calls=%async_computation.3 | async-start | bytes 12582912 | tf_op jit(solution)/shard_map/all_to_all | solution.py:93
  339.0 0.8 copy.56
  339.8 0.8 copy.55
  340.6 137.2 %all-to-all-done.2 = bf16[4,3,1,2048,128]{4,3,1,2,0:T(8,128)(2,1)} async-done(((bf16[4,3,1,2048,128]{4,3,1,2,0:T(8,128)(2,1)}), bf16[4,3,1,2048,128]{4,3,1,2,0:T(8,128)(2,1)}, u32[]{:S(2)}, u32[]{:S(2)}) %all-to-all-start.2) | async-done | bytes 6291488 | tf_op jit(solution)/shard_map/all_to_all | solution.py:93
  477.8 0.0 copy-done.5
  477.8 0.0 copy-start.1
  477.8 6.7 %fusion.8 = bf16[6,2048,128]{2,0,1:T(8,128)(2,1)S(1)} fusion(bf16[12,2048,128]{2,1,0:T(8,128)(2,1)} %bitcast.17, s32[12]{0:T(128)S(1)} %get-tuple-element.22, s32[12]{0:T(128)S(1)} %get-tuple-element.23, s32[6]{0:T(128)S(1)} %convert_reduce_fusion, s32[6]{0:T(128)S(1)} %copy-done.5), kind=kOutput, calls=%fused_computation.11 | convolution fusion | flops 39321816 | bytes 9437328 | tf_op jit(solution)/shard_map/sj,sdc->jdc/dot_general | solution.py:96
  484.5 2.1 copy.54
  486.5 0.0 copy-done.1
  (4 shorter events, 0.0 us)
Async XLA Ops:
  7.2 1.9 copy-start
  7.2 84.2 %reduce-scatter.2.cloned.1.call-start = ((), (), s32[]{:S(2)}) async-start(), calls=%async_computation.4 | async-start | bytes 7077888 | tf_op jit(solution)/shard_map/reduce_scatter | solution.py:49
  91.4 24.6 %all-to-all-start = ((bf16[4,3,256,128]{3,2,1,0:T(8,128)(2,1)}), bf16[4,3,256,128]{3,2,1,0:T(8,128)(2,1)S(1)}, u32[]{:S(2)}, u32[]{:S(2)}) async-start(bf16[4,3,256,128]{3,2,1,0:T(8,128)(2,1)} %bitcast.67), calls=%async_computation.1 | async-start | bytes 1572864 | tf_op jit(solution)/shard_map/all_to_all | solution.py:51
  117.7 24.5 %all-to-all-start.1 = ((bf16[8,3,256,128]{3,2,1,0:T(8,128)(2,1)}), bf16[8,3,256,128]{3,2,1,0:T(8,128)(2,1)S(1)}, u32[]{:S(2)}, u32[]{:S(2)}) async-start(bf16[8,3,256,128]{3,2,1,0:T(8,128)(2,1)} %fusion.7), calls=%async_computation.2 | async-start | bytes 3145728 | tf_op jit(solution)/shard_map/all_to_all | solution.py:58
  121.3 80.6 %all-reduce.2.cloned.1.call-start = ((), (), s32[]{:S(2)}) async-start(), calls=%async_computation.5 | async-start | bytes 1572864 | tf_op jit(solution)/shard_map/psum | solution.py:72
  144.0 4.8 copy-start.3
  144.0 4.9 %copy-start.4 = (f32[1,3,128,128]{3,2,1,0:T(8,128)S(1)}, f32[1,3,128,128]{3,2,1,0:T(8,128)}, u32[]{:S(2)}) copy-start(f32[1,3,128,128]{3,2,1,0:T(8,128)} %param.8) | copy-start | bytes 589828
  148.8 116.6 %all-gather.2.cloned.1.call-start = ((), (), s32[]{:S(2)}) async-start(), calls=%async_computation.6 | async-start | bytes 7077888 | tf_op jit(solution)/shard_map/all_gather | solution.py:90
  201.9 11.8 %copy-start.2 = (bf16[3,1024,128]{1,2,0:T(8,128)(2,1)S(1)}, bf16[3,1024,128]{1,2,0:T(8,128)(2,1)}, u32[]{:S(2)}) copy-start(bf16[3,1024,128]{1,2,0:T(8,128)(2,1)} %all-reduce.2.cloned.1.call-done) | copy-start | bytes 2359300
  333.6 144.2 %copy-start.5 = (s32[6]{0:T(128)S(1)}, s32[6]{0:T(128)}, u32[]{:S(2)}) copy-start(s32[6]{0:T(128)} %param.9) | copy-start | bytes 76
  333.6 144.2 %all-to-all-start.2 = ((bf16[4,3,1,2048,128]{4,3,1,2,0:T(8,128)(2,1)}), bf16[4,3,1,2048,128]{4,3,1,2,0:T(8,128)(2,1)}, u32[]{:S(2)}, u32[]{:S(2)}) async-start(bf16[4,3,1,2048,128]{4,3,1,2,0:T(8,128)(2,1)} %pad_maximum_fusion), calls=%async_computation.3 | async-start | bytes 12582912 | tf_op jit(solution)/shard_map/all_to_all | solution.py:93
  477.8 8.8 %copy-start.1 = (bf16[1,6,2048,128]{3,2,1,0:T(8,128)(2,1)S(1)}, bf16[1,6,2048,128]{3,2,1,0:T(8,128)(2,1)}, u32[]{:S(2)}) copy-start(bf16[1,6,2048,128]{3,2,1,0:T(8,128)(2,1)} %param.5) | copy-start | bytes 9437188
Sparse Core Ops, SparseCore 0:
  26.9 64.4 reduce-scatter.1
  148.9 52.9 all-reduce.1
  220.0 45.3 all-gather.1
